TPU v7x, 32 devices: a whole 2x2x4 slice. The times are simulated.
32 devices in a mesh: outer: 4 (over z), dev: 8 (over y, x, core).
Axes of the slice: x: 2, y: 2, z: 4, core: 2. Of those that a mesh axis runs over, the one named last changes fastest.
Arguments:
- partials: bfloat16 [32, 8192, 128], P(('outer', 'dev')), may hold values from -6 to 6
- p_old: bfloat16 [8192, 1024], P('dev'), may hold values from -0.0625 to 0.0625
- p_new: bfloat16 [8192, 1024], P('dev'), may hold values from -0.0625 to 0.0625
- weight: float32 [8192, 128], P('dev'), may hold values from -4 to 4
- m_old: float32 [1024, 128], P('dev'), may hold values from -96 to 96
- v_old: float32 [1024, 128], P('dev'), may hold values from 32 to 1280
Outputs:
- new_weight: float32 [8192, 128], P('dev')
- m_new: float32 [1024, 128], P('dev')
- v_new: float32 [1024, 128], P('dev')
All inputs are finite; a program needn't handle non-finite values.
Results may differ from a plain program's by a relative error of at most 0.0012.
Values may be sent and summed in bfloat16 or wider, within the bound.
A program may use at most 128 MiB of HBM per device.

v0:
```python
import jax
import jax.numpy as jnp
from jax import lax
from jax.sharding import PartitionSpec as P

beta_mean = 0.9
beta_square = 0.95
bias_mean = 0.9999734386011124
bias_square = 0.9940794707796659
adam_epsilon = 1e-08
step_scale = 0.5


def on_device(partials, p_old, p_new, weight, m_old, v_old):
    local_grad = partials[0].astype(jnp.float32)
    grad_rows = lax.psum_scatter(local_grad, "dev", scatter_dimension=0, tiled=True)
    basis = p_new.astype(jnp.float32)
    columns = basis
    projected = lax.psum_scatter(
        jnp.dot(columns.T, grad_rows, precision=lax.Precision.HIGHEST),
        "dev",
        scatter_dimension=0,
        tiled=True,
    )
    projected = lax.psum(projected, "outer")
    columns = p_new
    margin_rows = lax.psum_scatter(
        jnp.dot(columns.T, p_old, preferred_element_type=jnp.float32),
        "dev",
        scatter_dimension=0,
        tiled=True,
    )
    first_piece = lax.all_gather(m_old, "dev", axis=0, tiled=True)
    second_piece = lax.all_gather(v_old, "dev", axis=0, tiled=True)
    first = jnp.dot(margin_rows, first_piece, precision=lax.Precision.HIGHEST)
    second = jnp.dot(margin_rows * margin_rows, second_piece, precision=lax.Precision.HIGHEST)
    m_new = beta_mean * first + (1.0 - beta_mean) * projected
    v_new = beta_square * second + (1.0 - beta_square) * projected * projected
    direction = (m_new / bias_mean / (jnp.sqrt(v_new / bias_square) + adam_epsilon)).astype(
        jnp.bfloat16
    )
    columns = p_new
    update = jnp.dot(
        columns,
        lax.all_gather(direction, "dev", axis=0, tiled=True),
        preferred_element_type=jnp.float32,
    )
    new_weight = weight - step_scale * update
    return (new_weight, m_new, v_new)


def solution(mesh):
    in_specs = (
        P(("outer", "dev"), None, None),
        P("dev", None),
        P("dev", None),
        P("dev", None),
        P("dev", None),
        P("dev", None),
    )
    out_specs = (P("dev", None), P("dev", None), P("dev", None))
    return jax.shard_map(
        on_device, mesh=mesh, in_specs=in_specs, out_specs=out_specs, check_vma=False
    )
```

profile of v0, /device:TPU:0, one launch (start us, length us, event | category | flops | bytes accessed | tf_op | source)
XLA Modules:
  0.0 216.5 jit_solution(17691967801441322931)
XLA Ops:
  7.2 0.0 reduce-scatter.6.cloned.1.call-start
  7.2 3.9 %bitcast_convert_fusion = f32[8192,128]{1,0:T(8,128)} fusion(bf16[1,8192,128]{2,1,0:T(8,128)(2,1)} %param.6), kind=kLoop, calls=%fused_computation | loop fusion | flops 1048576 | bytes 6291456 | tf_op jit(solution)/shard_map/convert_element_type | solution.py:15
  11.2 0.0 reduce-scatter.6.cloned.1.call-update
  11.2 0.0 reduce-scatter.8.cloned.1.call-start
  11.2 54.0 %reduce-scatter.6.cloned.1.call-done = f32[1024,128]{1,0:T(8,128)} async-done(((f32[8192,128]{1,0:T(8,128)}), f32[1024,128]{1,0:T(8,128)}) %reduce-scatter.6.cloned.1.call-update) | async-done | bytes 524304 | tf_op jit(solution)/shard_map/reduce_scatter | solution.py:16
  65.3 4.1 %fusion.6 = f32[1024,128]{1,0:T(8,128)} fusion(bf16[1024,1024]{1,0:T(8,128)(2,1)S(1)} %copy-done, f32[1024,128]{1,0:T(8,128)} %reduce-scatter.6.cloned.1.call-done), kind=kOutput, calls=%fused_computation.12 | convolution fusion | flops 1610612736 | bytes 3145728 | tf_op jit(solution)/shard_map/dot_general | solution.py:20
  69.4 0.0 reduce-scatter.8.cloned.1.call-update
  69.5 0.0 reduce-scatter.4.cloned.1.call-start
  69.5 5.9 %fusion.5 = f32[1024,1024]{1,0:T(8,128)} fusion(bf16[1024,1024]{1,0:T(8,128)(2,1)S(1)} %copy-done, bf16[1024,1024]{1,0:T(8,128)(2,1)} %param.7), kind=kOutput, calls=%fused_computation.11 | convolution fusion | flops 2147483648 | bytes 8388608 | tf_op jit(solution)/shard_map/dot_general | solution.py:28
  75.4 0.0 reduce-scatter.4.cloned.1.call-update
  75.5 0.0 all-reduce.2.cloned.1.call-start
  75.5 1.0 copy-done.2
  76.5 1.0 copy.9
  77.5 9.8 %all_gather.9 = f32[1024,128]{1,0:T(8,128)S(1)} all-gather(f32[128,128]{1,0:T(8,128)S(1)} %copy-done.4), channel_id=1, replica_groups=mesh['outer'=4,'dev'=8] {'dev'}, dimensions={0}, use_global_device_ids=true | all-gather | bytes 589824 | tf_op jit(solution)/shard_map/all_gather | solution.py:33
  87.2 16.5 %reduce-scatter.8.cloned.1.call-done = f32[128,128]{1,0:T(8,128)} async-done(((f32[1024,128]{1,0:T(8,128)}), f32[128,128]{1,0:T(8,128)}) %reduce-scatter.8.cloned.1.call-update) | async-done | bytes 65552 | tf_op jit(solution)/shard_map/reduce_scatter | solution.py:19
  103.7 0.0 all-reduce.2.cloned.1.call-update
  103.8 9.8 %all_gather.10 = f32[1024,128]{1,0:T(8,128)S(1)} all-gather(f32[128,128]{1,0:T(8,128)S(1)} %copy-done.5), channel_id=1, replica_groups=mesh['outer'=4,'dev'=8] {'dev'}, dimensions={0}, use_global_device_ids=true | all-gather | bytes 589824 | tf_op jit(solution)/shard_map/all_gather | solution.py:34
  113.5 44.7 %reduce-scatter.4.cloned.1.call-done = f32[128,1024]{1,0:T(8,128)} async-done(((f32[1024,1024]{1,0:T(8,128)}), f32[128,1024]{1,0:T(8,128)}) %reduce-scatter.4.cloned.1.call-update) | async-done | bytes 524304 | tf_op jit(solution)/shard_map/reduce_scatter | solution.py:27
  158.3 36.5 %all-reduce.2.cloned.1.call-done = f32[128,128]{1,0:T(8,128)} async-done(((f32[128,128]{1,0:T(8,128)}), f32[128,128]{1,0:T(8,128)}) %all-reduce.2.cloned.1.call-update) | async-done | bytes 65552 | tf_op jit(solution)/shard_map/psum | solution.py:25
  194.8 1.7 fusion.3
  196.5 2.4 %divide_convert_fusion = (bf16[128,128]{1,0:T(8,128)(2,1)S(1)}, f32[128,128]{1,0:T(8,128)}) fusion(f32[128,128]{1,0:T(8,128)S(1)} %fusion.3, f32[128,128]{1,0:T(8,128)} %all-reduce.2.cloned.1.call-done, f32[1024,128]{1,0:T(8,128)S(1)} %all_gather.10, f32[128,1024]{1,0:T(8,128)} %reduce-scatter.4.cloned.1.call-done), kind=kOutput, calls=%fused_computation.10 | convolution fusion | flops 201605120 | bytes 1277952 | tf_op jit(solution)/shard_map/dot_general | solution.py:36
  198.9 9.2 %all_gather.11 = bf16[1024,128]{1,0:T(8,128)(2,1)S(1)} all-gather(bf16[128,128]{1,0:T(8,128)(2,1)S(1)} %get-tuple-element.6), channel_id=1, replica_groups=mesh['outer'=4,'dev'=8] {'dev'}, dimensions={0}, use_global_device_ids=true | all-gather | bytes 294912 | tf_op jit(solution)/shard_map/all_gather | solution.py:45
  208.1 0.8 fusion.1
  209.0 1.0 copy.10
  (11 shorter events, 0.0 us)
Async XLA Ops:
  7.2 58.1 %copy-start = (bf16[1024,1024]{1,0:T(8,128)(2,1)S(1)}, bf16[1024,1024]{1,0:T(8,128)(2,1)}, u32[]{:S(2)}) copy-start(bf16[1024,1024]{1,0:T(8,128)(2,1)} %param.8) | copy-start | bytes 6291460
  7.2 58.1 %reduce-scatter.6.cloned.1.call-start = ((), (), s32[]{:S(2)}) async-start(), calls=%async_computation.4 | async-start | bytes 4718592 | tf_op jit(solution)/shard_map/reduce_scatter | solution.py:16
  11.2 92.5 %reduce-scatter.8.cloned.1.call-start = ((), (), s32[]{:S(2)}) async-start(), calls=%async_computation.5 | async-start | bytes 589824 | tf_op jit(solution)/shard_map/reduce_scatter | solution.py:19
  69.5 88.8 %reduce-scatter.4.cloned.1.call-start = ((), (), s32[]{:S(2)}) async-start(), calls=%async_computation.3 | async-start | bytes 4718592 | tf_op jit(solution)/shard_map/reduce_scatter | solution.py:27
  75.4 1.0 copy-start.2
  75.4 2.0 copy-start.4
  75.4 28.3 %copy-start.5 = (f32[128,128]{1,0:T(8,128)S(1)}, f32[128,128]{1,0:T(8,128)}, u32[]{:S(2)}) copy-start(f32[128,128]{1,0:T(8,128)} %param.11) | copy-start | bytes 196612
  75.5 119.3 %all-reduce.2.cloned.1.call-start = ((), (), s32[]{:S(2)}) async-start(), calls=%async_computation.6 | async-start | bytes 131072 | tf_op jit(solution)/shard_map/psum | solution.py:25
  194.8 13.4 %copy-start.1 = (f32[1024,128]{0,1:T(8,128)S(1)}, f32[1024,128]{0,1:T(8,128)}, u32[]{:S(2)}) copy-start(f32[1024,128]{0,1:T(8,128)} %copy.9) | copy-start | bytes 1572868
  196.5 12.5 %copy-start.3 = (f32[128,128]{1,0:T(8,128)}, f32[128,128]{1,0:T(8,128)S(1)}, u32[]{:S(2)}) copy-start(f32[128,128]{1,0:T(8,128)S(1)} %fusion.3) | copy-start | bytes 196612
Sparse Core Ops, SparseCore 0:
  11.3 53.8 reduce-scatter.5
  69.6 34.0 reduce-scatter.7
  107.1 51.1 reduce-scatter.3
  160.5 34.2 all-reduce.1
where the time goes:
time: 217 us
  waiting for transfers between devices  152 us (70%)
  blocking collectives  28.8 us (13%)
  matrix products  15 us (7%)
  between operations  13.8 us (6%)
  other arithmetic  3.94 us (2%)
  local copies, waits for them, and re-layouts  2.99 us (1%)
    reduce_scatter x1, waiting for transfers between devices, on_device(): lax.psum_scatter(local_grad, 'dev', scatter_dimension=0, tiled=True)  54 us
    reduce_scatter x1, waiting for transfers between devices, on_device(): lax.psum_scatter(jnp.dot(columns.T, p_old, preferred_element_type=jnp.flo...  44.7 us
    psum x1, waiting for transfers between devices, on_device(): projected = lax.psum(projected, 'outer')  36.5 us
    reduce_scatter x1, waiting for transfers between devices, on_device(): lax.psum_scatter(jnp.dot(columns.T, grad_rows, precision=lax.Precision.HI...  16.5 us
    all_gather x1, blocking collectives, on_device(): second_piece = lax.all_gather(v_old, 'dev', axis=0, tiled=True)  9.79 us
    all_gather x1, blocking collectives, on_device(): first_piece = lax.all_gather(m_old, 'dev', axis=0, tiled=True)  9.77 us
    all_gather x1, blocking collectives, on_device(): lax.all_gather(direction, 'dev', axis=0, tiled=True)  9.25 us
    dot_general x1, matrix products, on_device(): jnp.dot(columns.T, p_old, preferred_element_type=jnp.float32)  5.92 us
  transfers between devices with their start and end apart: 4, of which 4 were waited for; matrix products, arithmetic and copies ran while one was open for 3% of the time, Pallas kernels for 0%

commit v1 on v0

--- a/solution.py
+++ b/solution.py
@@ -22,7 +22,8 @@
         scatter_dimension=0,
         tiled=True,
     )
-    projected = lax.psum(projected, "outer")
+    parts = lax.all_gather(projected, "outer", axis=0, tiled=False)
+    projected = parts.sum(axis=0)
     columns = p_new
     margin_rows = lax.psum_scatter(
         jnp.dot(columns.T, p_old, preferred_element_type=jnp.float32),

time: 217 us -> 181 us (0.83)
  waiting for transfers between devices: 152 us -> 102 us
  blocking collectives: 28.8 us -> 42.6 us
    psum x1 -> x0, waiting for transfers between devices: 36.5 us -> none  [on_device(): projected = lax.psum(projected, 'outer')]
    all_gather x0 -> x1, blocking collectives: none -> 14 us  [on_device(): parts = lax.all_gather(projected, 'outer', axis=0, tiled=False)]
    reduce_scatter x1, waiting for transfers between devices: 16.5 us -> 7.43 us  [on_device(): lax.psum_scatter(jnp.dot(columns.T, grad_rows, precision=lax.Precision.HI...]
    reduce_scatter x1, waiting for transfers between devices: 44.7 us -> 40.5 us  [on_device(): lax.psum_scatter(jnp.dot(columns.T, p_old, preferred_element_type=jnp.flo...]
  transfers between devices with their start and end apart: 4 -> 3, of which waited for: 4 -> 3; matrix products, arithmetic and copies ran while one was open for 3% -> 4% of each run, Pallas kernels for 0% -> 0%
where the time goes in v1:
time: 181 us
  waiting for transfers between devices  102 us (56%)
  blocking collectives  42.6 us (24%)
  matrix products  15 us (8%)
  between operations  13.8 us (8%)
  other arithmetic  3.95 us (2%)
  local copies, waits for them, and re-layouts  3.04 us (2%)
    reduce_scatter x1, waiting for transfers between devices, on_device(): lax.psum_scatter(local_grad, 'dev', scatter_dimension=0, tiled=True)  54.1 us
    reduce_scatter x1, waiting for transfers between devices, on_device(): lax.psum_scatter(jnp.dot(columns.T, p_old, preferred_element_type=jnp.flo...  40.5 us
    all_gather x1, blocking collectives, on_device(): parts = lax.all_gather(projected, 'outer', axis=0, tiled=False)  14 us
    all_gather x1, blocking collectives, on_device(): first_piece = lax.all_gather(m_old, 'dev', axis=0, tiled=True)  9.77 us
    all_gather x1, blocking collectives, on_device(): second_piece = lax.all_gather(v_old, 'dev', axis=0, tiled=True)  9.58 us
    all_gather x1, blocking collectives, on_device(): lax.all_gather(direction, 'dev', axis=0, tiled=True)  9.23 us
    reduce_scatter x1, waiting for transfers between devices, on_device(): lax.psum_scatter(jnp.dot(columns.T, grad_rows, precision=lax.Precision.HI...  7.43 us
    dot_general x1, matrix products, on_device(): jnp.dot(columns.T, p_old, preferred_element_type=jnp.float32)  5.91 us
  transfers between devices with their start and end apart: 3, of which 3 were waited for; matrix products, arithmetic and copies ran while one was open for 4% of the time, Pallas kernels for 0%

profile of v1, /device:TPU:0, one launch (start us, length us, event | category | flops | bytes accessed | tf_op | source)
XLA Modules:
  0.0 180.6 jit_solution(1117037717697461161)
XLA Ops:
  7.2 0.0 copy-start
  7.2 0.0 reduce-scatter.6.cloned.1.call-start
  7.2 3.9 %bitcast_convert_fusion = f32[8192,128]{1,0:T(8,128)} fusion(bf16[1,8192,128]{2,1,0:T(8,128)(2,1)} %param.6), kind=kLoop, calls=%fused_computation | loop fusion | flops 1048576 | bytes 6291456 | tf_op jit(solution)/shard_map/convert_element_type | solution.py:15
  11.2 0.0 reduce-scatter.6.cloned.1.call-update
  11.2 0.0 reduce-scatter.8.cloned.1.call-start
  11.2 54.1 %reduce-scatter.6.cloned.1.call-done = f32[1024,128]{1,0:T(8,128)} async-done(((f32[8192,128]{1,0:T(8,128)}), f32[1024,128]{1,0:T(8,128)}) %reduce-scatter.6.cloned.1.call-update) | async-done | bytes 524304 | tf_op jit(solution)/shard_map/reduce_scatter | solution.py:16
  65.3 4.2 %fusion.6 = f32[1024,128]{1,0:T(8,128)} fusion(bf16[1024,1024]{1,0:T(8,128)(2,1)S(1)} %copy-done, f32[1024,128]{1,0:T(8,128)} %reduce-scatter.6.cloned.1.call-done), kind=kOutput, calls=%fused_computation.12 | convolution fusion | flops 1610612736 | bytes 3145728 | tf_op jit(solution)/shard_map/dot_general | solution.py:20
  69.5 0.0 reduce-scatter.8.cloned.1.call-update
  69.5 0.0 reduce-scatter.4.cloned.1.call-start
  69.5 5.9 %fusion.5 = f32[1024,1024]{1,0:T(8,128)} fusion(bf16[1024,1024]{1,0:T(8,128)(2,1)S(1)} %copy-done, bf16[1024,1024]{1,0:T(8,128)(2,1)} %param.7), kind=kOutput, calls=%fused_computation.11 | convolution fusion | flops 2147483648 | bytes 8388608 | tf_op jit(solution)/shard_map/dot_general | solution.py:29
  75.5 0.0 reduce-scatter.4.cloned.1.call-update
  75.5 1.0 copy-done.2
  76.5 1.0 copy.9
  77.5 9.8 %all_gather.15 = f32[1024,128]{1,0:T(8,128)S(1)} all-gather(f32[128,128]{1,0:T(8,128)S(1)} %copy-done.4), channel_id=1, replica_groups=mesh['outer'=4,'dev'=8] {'dev'}, dimensions={0}, use_global_device_ids=true | all-gather | bytes 589824 | tf_op jit(solution)/shard_map/all_gather | solution.py:34
  87.3 9.6 %all_gather.18 = f32[1024,128]{1,0:T(8,128)S(1)} all-gather(f32[128,128]{1,0:T(8,128)S(1)} %copy-done.5), channel_id=1, replica_groups=mesh['outer'=4,'dev'=8] {'dev'}, dimensions={0}, use_global_device_ids=true | all-gather | bytes 589824 | tf_op jit(solution)/shard_map/all_gather | solution.py:35
  96.8 7.4 %reduce-scatter.8.cloned.1.call-done = f32[128,128]{1,0:T(8,128)} async-done(((f32[1024,128]{1,0:T(8,128)}), f32[128,128]{1,0:T(8,128)}) %reduce-scatter.8.cloned.1.call-update) | async-done | bytes 65552 | tf_op jit(solution)/shard_map/reduce_scatter | solution.py:19
  104.3 14.0 %all-gather = f32[512,128]{1,0:T(8,128)S(1)} all-gather(f32[128,128]{1,0:T(8,128)} %reduce-scatter.8.cloned.1.call-done), channel_id=2, replica_groups=mesh['outer'=4,'dev'=8] {'outer'}, dimensions={0}, use_global_device_ids=true | all-gather | bytes 327680 | tf_op jit(solution)/shard_map/all_gather | solution.py:25
  118.3 40.5 %reduce-scatter.4.cloned.1.call-done = f32[128,1024]{1,0:T(8,128)} async-done(((f32[1024,1024]{1,0:T(8,128)}), f32[128,1024]{1,0:T(8,128)}) %reduce-scatter.4.cloned.1.call-update) | async-done | bytes 524304 | tf_op jit(solution)/shard_map/reduce_scatter | solution.py:28
  158.8 1.7 fusion.3
  160.6 0.0 copy-start.3
  160.6 2.4 %divide_convert_fusion = (bf16[128,128]{1,0:T(8,128)(2,1)S(1)}, f32[128,128]{1,0:T(8,128)}) fusion(f32[128,128]{1,0:T(8,128)S(1)} %fusion.3, f32[128,128]{1,0:T(8,128)S(1)} %reduce_sum.9, f32[1024,128]{1,0:T(8,128)S(1)} %all_gather.18, f32[128,1024]{1,0:T(8,128)} %reduce-scatter.4.cloned.1.call-done), kind=kOutput, calls=%fused_computation.10 | convolution fusion | flops 201605120 | bytes 1277952 | tf_op jit(solution)/shard_map/dot_general | solution.py:37
  162.9 9.2 %all_gather.19 = bf16[1024,128]{1,0:T(8,128)(2,1)S(1)} all-gather(bf16[128,128]{1,0:T(8,128)(2,1)S(1)} %get-tuple-element.6), channel_id=1, replica_groups=mesh['outer'=4,'dev'=8] {'dev'}, dimensions={0}, use_global_device_ids=true | all-gather | bytes 294912 | tf_op jit(solution)/shard_map/all_gather | solution.py:46
  172.2 0.8 fusion.1
  173.0 1.0 copy.10
  (10 shorter events, 0.0 us)
Async XLA Ops:
  7.2 58.1 %copy-start = (bf16[1024,1024]{1,0:T(8,128)(2,1)S(1)}, bf16[1024,1024]{1,0:T(8,128)(2,1)}, u32[]{:S(2)}) copy-start(bf16[1024,1024]{1,0:T(8,128)(2,1)} %param.8) | copy-start | bytes 6291460
  7.2 58.1 %reduce-scatter.6.cloned.1.call-start = ((), (), s32[]{:S(2)}) async-start(), calls=%async_computation.4 | async-start | bytes 4718592 | tf_op jit(solution)/shard_map/reduce_scatter | solution.py:16
  11.2 93.1 %reduce-scatter.8.cloned.1.call-start = ((), (), s32[]{:S(2)}) async-start(), calls=%async_computation.5 | async-start | bytes 589824 | tf_op jit(solution)/shard_map/reduce_scatter | solution.py:19
  69.5 89.4 %reduce-scatter.4.cloned.1.call-start = ((), (), s32[]{:S(2)}) async-start(), calls=%async_computation.3 | async-start | bytes 4718592 | tf_op jit(solution)/shard_map/reduce_scatter | solution.py:28
  75.5 1.0 copy-start.2
  75.5 2.0 %copy-start.4 = (f32[128,128]{1,0:T(8,128)S(1)}, f32[128,128]{1,0:T(8,128)}, u32[]{:S(2)}) copy-start(f32[128,128]{1,0:T(8,128)} %param.10) | copy-start | bytes 196612
  75.5 11.8 %copy-start.5 = (f32[128,128]{1,0:T(8,128)S(1)}, f32[128,128]{1,0:T(8,128)}, u32[]{:S(2)}) copy-start(f32[128,128]{1,0:T(8,128)} %param.11) | copy-start | bytes 196612
  158.8 13.3 %copy-start.1 = (f32[1024,128]{0,1:T(8,128)S(1)}, f32[1024,128]{0,1:T(8,128)}, u32[]{:S(2)}) copy-start(f32[1024,128]{0,1:T(8,128)} %copy.9) | copy-start | bytes 1572868
  160.6 12.5 %copy-start.3 = (f32[128,128]{1,0:T(8,128)}, f32[128,128]{1,0:T(8,128)S(1)}, u32[]{:S(2)}) copy-start(f32[128,128]{1,0:T(8,128)S(1)} %fusion.3) | copy-start | bytes 196612
Sparse Core Ops, SparseCore 0:
  11.3 53.8 reduce-scatter.5
  69.6 34.6 reduce-scatter.7
  107.6 51.1 reduce-scatter.3
